TPU v7x, 256 devices: a whole 4x4x8 slice. The times are simulated.
256 devices in a mesh: kx: 8 (over z), ht: 8 (over y, core), real: 4 (over x).
Axes of the slice: x: 4, y: 4, z: 8, core: 2. Of those that a mesh axis runs over, the one named last changes fastest.
Arguments:
- velocity: float32 [3, 4, 32, 512, 128], P(None, 'real', 'kx', 'ht'), may hold values from -6 to 6
- low_index: int32 [8], replicated, may hold values from 0 to 31, as said below
- neighbours: int32 [32, 8], P('kx'), may hold values from 0 to 31, as said below
- owner_map: int32 [64], replicated, may hold values from 0 to 63, each once
- mode_counts: int32 [32], P('kx'), may hold values from 16 to 64
- helmholtz: float32 [64, 512, 512], P(('kx', 'ht')), may hold values from -0.25 to 0.25
Outputs:
- velocity_next: float32 [3, 4, 32, 512, 128], P(None, 'real', 'kx', 'ht')
Inputs may be any that keep to these rules, and one draw needn't show every extreme that they name: `low_index`: distinct values. neighbours[m, j] lies within 4 modes of m, counting circularly over the 32 modes; offsets of + 4 and - 4 both occur.
All inputs are finite; a program needn't handle non-finite values.
Results may differ from a plain program's by a relative error of at most 0.0001.
Values sent between devices are 32-bit elements; how exact they have to be, the bound alone decides.
A program may use at most 64 MiB of HBM per device.

v0:
```python
import jax
import jax.numpy as jnp
from jax import lax
from jax.sharding import PartitionSpec as P

dt_step = 0.1


def extended_2(block, sides, width):
    for axis, dim in sides:
        count = lax.axis_size(axis)
        forward = [(i, i + 1) for i in range(count - 1)]
        forward.append((count - 1, 0))
        backward = [(target, source) for source, target in forward]
        low = lax.ppermute(
            lax.slice_in_dim(block, block.shape[dim] - width, None, axis=dim), axis, forward
        )
        high = lax.ppermute(lax.slice_in_dim(block, 0, width, axis=dim), axis, backward)
        block = jnp.concatenate([low, block, high], axis=dim)
    return block


def spanwise_tables(mode_count, point_count):
    column_ids = jnp.arange(2 * mode_count)
    wavenumber = (column_ids // 2).astype(jnp.float32)
    imag_part = column_ids % 2
    positions = 2.0 * jnp.pi * jnp.arange(point_count).astype(jnp.float32) / point_count
    phases = wavenumber[:, None] * positions[None, :]
    forward = jnp.where(imag_part[:, None] == 0, jnp.cos(phases), -jnp.sin(phases)) / jnp.sqrt(
        jnp.float32(mode_count)
    )
    backward = forward.T * (2.0 * mode_count / point_count)
    return (forward, backward)


def apply_inverse(block, helmholtz, kx_count, ht_count, slots_dev, rows_ht):
    components, reals_dev, band_modes = (block.shape[0], block.shape[1], block.shape[2])
    regrouped = block.reshape(
        components, reals_dev, band_modes, kx_count, ht_count, slots_dev, 2, rows_ht
    )
    regrouped = regrouped.transpose(0, 1, 3, 2, 5, 6, 4, 7)
    regrouped = regrouped.reshape(
        components, reals_dev, kx_count * band_modes, slots_dev, 2, ht_count * rows_ht
    )
    solved = jnp.einsum("syx,crmspx->crmspy", helmholtz, regrouped, precision=lax.Precision.HIGHEST)
    solved = solved.reshape(
        components, reals_dev, kx_count, band_modes, slots_dev, 2, ht_count, rows_ht
    )
    solved = solved.transpose(0, 1, 3, 2, 6, 4, 5, 7)
    return solved.reshape(block.shape)


def local(velocity, low_index, neighbours, owner_map, mode_counts, helmholtz):
    highest = lax.Precision.HIGHEST
    components, reals_dev, band_modes, rows_ht, columns = velocity.shape
    kz_modes = columns // 2
    forward, backward = spanwise_tables(kz_modes, 4 * kz_modes)
    kx_count = lax.axis_size("kx")
    ht_count = lax.axis_size("ht")
    kx_total = band_modes * kx_count
    realizations = reals_dev * lax.axis_size("real")
    owners = kx_count * ht_count
    slots_dev = kz_modes // owners
    width_out = slots_dev * 2 * rows_ht
    low_members = low_index.shape[0]
    band_start = lax.axis_index("kx") * band_modes
    global_modes = band_start + jnp.arange(band_modes, dtype=jnp.int32)
    low_select = (low_index[:, None] == global_modes[None, :]).astype(jnp.float32)
    high_mask = 1.0 - jnp.sum(low_select, axis=0)
    offsets = (neighbours - global_modes[:, None] + kx_total // 2) % kx_total - kx_total // 2
    local_partner = jnp.arange(band_modes, dtype=jnp.int32)[:, None] + band_modes + offsets
    column_mask = ((jnp.arange(columns) // 2)[None, :] < mode_counts[:, None]).astype(jnp.float32)
    inverse_map = (
        jnp.zeros((kz_modes,), jnp.int32).at[owner_map].set(jnp.arange(kz_modes, dtype=jnp.int32))
    )
    current = velocity
    physical = jnp.dot(current, forward, precision=highest)
    extended = extended_2(physical, (("kx", 2),), band_modes)
    own_low = jnp.einsum("jm,crmyz->crjyz", low_select, physical, precision=highest)
    low_fields = lax.psum(own_low, "kx")
    high_low = jnp.zeros_like(physical)
    stresses = []
    for member in range(low_members):
        partner = jnp.take(extended, local_partner[:, member], axis=2)
        low_one = low_fields[:, :, member : member + 1]
        high_low = high_low + low_one * partner[1:2] + partner * low_one[1:2]
        weighted = physical * (partner[1:2] * high_mask[None, None, :, None, None])
        stresses.append(jnp.sum(weighted, axis=(1, 2)))
    stress = jnp.stack(stresses, axis=1)
    nonlinear = jnp.dot(high_low, backward, precision=highest)
    summed = lax.psum(stress, ("kx", "real"))
    low_forcing = jnp.dot(summed / realizations, backward, precision=highest)
    forcing = nonlinear * high_mask[None, None, :, None, None]
    forcing = (
        forcing + jnp.einsum("jm,cjyk->cmyk", low_select, low_forcing, precision=highest)[:, None]
    )
    forcing = forcing * column_mask[None, None, :, None, :]
    updated = current + dt_step * forcing
    slotted = jnp.take(
        updated.reshape(components, reals_dev, band_modes, rows_ht, kz_modes, 2), owner_map, axis=4
    )
    outgoing = slotted.reshape(components, reals_dev, band_modes, rows_ht, owners, slots_dev, 2)
    outgoing = outgoing.transpose(0, 1, 2, 4, 5, 6, 3)
    flat_out = outgoing.reshape(components, reals_dev, band_modes, owners, width_out)
    applied = apply_inverse(
        lax.all_to_all(flat_out, ("kx", "ht"), split_axis=3, concat_axis=3, tiled=True),
        helmholtz,
        kx_count,
        ht_count,
        slots_dev,
        rows_ht,
    )
    returned = lax.all_to_all(applied, ("kx", "ht"), split_axis=3, concat_axis=3, tiled=True)
    restored = returned.reshape(components, reals_dev, band_modes, owners, slots_dev, 2, rows_ht)
    restored = restored.transpose(0, 1, 2, 6, 3, 4, 5).reshape(
        components, reals_dev, band_modes, rows_ht, kz_modes, 2
    )
    current = jnp.take(restored, inverse_map, axis=4).reshape(
        components, reals_dev, band_modes, rows_ht, columns
    )
    return current


def solution(mesh):
    in_specs = (
        P(None, "real", "kx", "ht", None),
        P(),
        P("kx", None),
        P(),
        P("kx"),
        P(("kx", "ht"), None, None),
    )
    out_specs = P(None, "real", "kx", "ht", None)
    return jax.shard_map(local, mesh=mesh, in_specs=in_specs, out_specs=out_specs, check_vma=False)
```

profile of v0, /device:TPU:1, one launch (start us, length us, event | category | flops | bytes accessed | tf_op | source)
XLA Modules:
  0.0 327.1 jit_solution(15920989410416831472)
XLA Ops:
  6.6 2.4 fusion.12
  9.0 2.5 collective-permute-start
  11.5 4.0 %collective-permute-start.1 = (f32[3,1,4,64,256]{4,3,2,0,1:T(8,128)S(1)}, f32[3,1,4,64,256]{4,3,2,0,1:T(8,128)}, u32[]{:S(2)}, u32[]{:S(2)}) collective-permute-start(f32[3,1,4,64,256]{4,3,2,0,1:T(8,128)S(1)} %bitcast.259), channel_id=1, source_target_pairs={{32,0},{64,32},{96,64},{128,96},{160,128},{192,160},{224,192},{0,2... | collective-permute-start | bytes 2359304 | tf_op jit(solution)/shard_map/ppermute | solution.py:18
  15.6 3.1 convolution_bitcast_fusion
  19.8 12.9 %collective-permute-done = f32[3,1,4,64,256]{4,3,2,0,1:T(8,128)S(1)} collective-permute-done((f32[3,1,4,64,256]{4,3,2,0,1:T(8,128)S(1)}, f32[3,1,4,64,256]{4,3,2,0,1:T(8,128)S(1)}, u32[]{:S(2)}, u32[]{:S(2)}) %collective-permute-start) | collective-permute-done | bytes 786464 | tf_op jit(solution)/shard_map/ppermute | solution.py:15
  32.7 0.9 copy-done.16
  33.6 1.8 maximum_bitcast_fusion
  35.4 1.6 gather_fusion.7
  37.0 1.5 gather_fusion.5
  38.5 1.5 gather_fusion.4
  40.0 1.5 gather_fusion.3
  41.5 1.5 gather_fusion.2
  43.0 1.5 gather_fusion.1
  44.5 1.5 gather_fusion
  46.0 1.5 gather_fusion.6
  47.5 1.4 bitcast_select_fusion.2
  48.9 1.3 bitcast_select_fusion.4
  50.8 0.6 copy-done.10
  52.1 1.4 multiply_bitcast_fusion.1
  55.4 3.9 %stack.35 = f32[3,8,64,256]{3,1,2,0:T(8,128)} concatenate(f32[3,1,64,256]{3,1,2,0:T(1,128)S(1)} %stack.27, f32[3,1,64,256]{3,1,2,0:T(1,128)S(1)} %stack.28, f32[3,1,64,256]{3,1,2,0:T(1,128)S(1)} %stack.29, f32[3,1,64,256]{3,1,2,0:T(1,128)S(1)} %stack.30, f32[3,1,64,256]{3,1,2,0:T(1,128)S(1)} %stack.31, f32[3,1,64,256]{3,1,2,0:T(1,128)S(1)} %stack.32, ...), dimensions={1} | concatenate | bytes 3145728 | tf_op jit(solution)/shard_map/stack | solution.py:89
  60.4 35.1 %all-reduce.3.cloned.1.call-done = f32[3,1,8,64,256]{4,2,3,0,1:T(8,128)} async-done(((f32[3,1,8,64,256]{4,2,3,0,1:T(8,128)}), f32[3,1,8,64,256]{4,2,3,0,1:T(8,128)}) %all-reduce.3.cloned.1.call-update) | async-done | bytes 1572880 | tf_op jit(solution)/shard_map/psum | solution.py:80
  95.5 7.7 %fusion.51 = (f32[3,1,1,64,256]{4,2,3,0,1:T(1,128)S(1)}, f32[3,1,1,64,256]{4,2,3,0,1:T(1,128)S(1)}, f32[3,1,1,64,256]{4,2,3,0,1:T(1,128)S(1)}, f32[3,1,1,64,256]...) fusion(f32[3,1,8,64,256]{4,2,3,0,1:T(8,128)} %all-reduce.3.clon, ...), kind=kLoop, calls=%fused_computation.172 | loop fusion | bytes 3145728 | tf_op jit(solution)/shard_map/slice | solution.py:85
  103.2 0.7 copy.102
  103.8 0.7 copy.103
  104.5 0.7 copy.104
  105.2 0.7 copy.105
  105.9 0.7 copy.106
  106.6 0.7 copy.107
  107.3 0.7 copy.108
  108.0 0.7 copy.109
  108.7 3.5 %fusion.52 = (f32[1,1,1,64,256]{4,2,3,0,1:T(1,128)S(1)}, f32[1,1,1,64,256]{4,2,3,0,1:T(1,128)S(1)}, f32[1,1,1,64,256]{4,2,3,0,1:T(1,128)S(1)}, f32[1,1,1,64,256]...) fusion(f32[3,1,8,64,256]{4,2,3,0,1:T(8,128)} %all-reduce.3.clon, ...), kind=kLoop, calls=%fused_computation.173 | loop fusion | bytes 1048576 | tf_op jit(solution)/shard_map/slice | solution.py:86
  112.2 0.6 copy.112
  113.5 0.6 copy.114
  115.3 0.6 copy.117
  116.0 133.7 %all-reduce.5.cloned.1.call-done = f32[3,8,64,256]{3,1,2,0:T(8,128)} async-done(((f32[3,8,64,256]{3,1,2,0:T(8,128)}), f32[3,8,64,256]{3,1,2,0:T(8,128)}) %all-reduce.5.cloned.1.call-update) | async-done | bytes 1572880 | tf_op jit(solution)/shard_map/psum | solution.py:91
  249.7 3.5 %fusion = f32[3,8,64,128]{3,1,2,0:T(8,128)S(1)} fusion(f32[3,8,64,256]{3,1,2,0:T(8,128)} %all-reduce.5.cloned.1.call-done, f32[256]{0:T(256)S(1)} %convert_multiply_fusion, f32[128]{0:T(128)} %copy-done.17, pred[128]{0:T(512)(128)(4,1)S(1)} %fusion.42), kind=kOutput, calls=%fused_computation.12 | convolution fusion | flops 604504064 | bytes 2360960 | tf_op jit(solution)/shard_map/dot_general | solution.py:92
  253.2 1.2 fusion.50
  254.4 5.9 %fusion.6 = f32[3,1,4,64,128]{4,3,2,0,1:T(8,128)} fusion(f32[3,1,4,64,128]{4,3,2,1,0:T(8,128)S(1)} %copy-done.14, f32[3,64,128,4]{2,3,1,0:T(4,128)S(1)} %fusion.50, f32[4,128]{1,0:T(4,128)S(1)} %compare_convert_fusion.1, f32[4]{0:T(128)} %copy-done.27, f32[256]{0:T(256)S(1)} %convert_multiply_fusion, f32[128]{0:T(128)} %copy-done.17, ...), kind=kOutput, calls=%fused_computation.21 | convolution fusion | flops 310280192 | bytes 11669168 | tf_op jit(solution)/shard_map/dot_general | solution.py:90
  260.3 1.3 copy.38
  262.1 1.0 gather_fusion.8
  264.4 27.5 %all_to_all.10 = f32[3,1,4,64,128]{4,2,0,1,3:T(4,128)S(1)} all-to-all(f32[3,1,4,64,128]{4,2,0,1,3:T(4,128)S(1)} %reshape.457), channel_id=1, replica_groups=mesh['kx'=8,'ht'=8,'real'=4] {'kx','ht'}, dimensions={3} | all-to-all | bytes 786432 | tf_op jit(solution)/shard_map/all_to_all | solution.py:106
  292.8 1.5 convolution_bitcast_fusion.1
  294.9 1.3 reshape.459
  296.2 5.5 %all-to-all-start.1 = ((f32[3,1,4,64,128]{4,2,0,1,3:T(4,128)}), f32[3,1,4,64,128]{4,2,0,1,3:T(4,128)S(1)}, u32[]{:S(2)}, u32[]{:S(2)}) async-start(f32[3,1,4,64,128]{4,2,0,1,3:T(4,128)} %reshape.459), calls=%async_computation.1 | async-start | bytes 786432 | tf_op jit(solution)/shard_map/all_to_all | solution.py:113
  301.6 0.9 scatter_custom_fusion
  302.6 14.2 %all-to-all-done.1 = f32[3,1,4,64,128]{4,2,0,1,3:T(4,128)S(1)} async-done(((f32[3,1,4,64,128]{4,2,0,1,3:T(4,128)}), f32[3,1,4,64,128]{4,2,0,1,3:T(4,128)S(1)}, u32[]{:S(2)}, u32[]{:S(2)}) %all-to-all-start.1) | async-done | bytes 393248 | tf_op jit(solution)/shard_map/all_to_all | solution.py:113
  317.5 1.1 gather_fusion.9
  319.3 1.0 copy.49
  (145 shorter events, 11.2 us)
Async XLA Ops:
  6.5 286.2 %copy-start = (f32[1,512,512]{2,1,0:T(8,128)S(1)}, f32[1,512,512]{2,1,0:T(8,128)}, u32[]{:S(2)}) copy-start(f32[1,512,512]{2,1,0:T(8,128)} %param.15) | copy-start | bytes 3145732
  6.5 89.0 %all-reduce.3.cloned.1.call-start = ((), (), s32[]{:S(2)}) async-start(), calls=%async_computation.2 | async-start | bytes 3145728 | tf_op jit(solution)/shard_map/psum | solution.py:80
  6.6 12.2 %copy-start.17 = (f32[128]{0:T(128)}, f32[128]{0:T(128)S(1)}, u32[]{:S(2)}) copy-start(f32[128]{0:T(128)S(1)} %fusion.45) | copy-start | bytes 1540
  6.6 12.2 %copy-start.28 = (s32[4,8]{1,0:T(4,128)S(1)}, s32[4,8]{1,0:T(4,128)}, u32[]{:S(2)}) copy-start(s32[4,8]{1,0:T(4,128)} %param.12) | copy-start | bytes 388
  6.6 13.0 %copy-start.29 = (s32[8]{0:T(128)S(1)}, s32[8]{0:T(128)}, u32[]{:S(2)}) copy-start(s32[8]{0:T(128)} %param.11) | copy-start | bytes 100
  9.0 23.7 %copy-start.1 = (f32[256,3,4,64]{0,3,2,1:T(8,128)}, f32[256,3,4,64]{0,3,2,1:T(8,128)S(1)}, u32[]{:S(2)}) copy-start(f32[256,3,4,64]{0,3,2,1:T(8,128)S(1)} %fusion.12) | copy-start | bytes 2359300
  9.0 23.7 %collective-permute-start = (f32[3,1,4,64,256]{4,3,2,0,1:T(8,128)S(1)}, f32[3,1,4,64,256]{4,3,2,0,1:T(8,128)S(1)}, u32[]{:S(2)}, u32[]{:S(2)}) collective-permute-start(f32[3,1,4,64,256]{4,3,2,0,1:T(8,128)S(1)} %bitcast.258), channel_id=1, source_target_pairs={{0,32},{32,64},{64,96},{96,128},{128,160},{160,192},{192,224},{224... | collective-permute-start | bytes 2359304 | tf_op jit(solution)/shard_map/ppermute | solution.py:15
  11.5 22.1 %collective-permute-start.1 = (f32[3,1,4,64,256]{4,3,2,0,1:T(8,128)S(1)}, f32[3,1,4,64,256]{4,3,2,0,1:T(8,128)}, u32[]{:S(2)}, u32[]{:S(2)}) collective-permute-start(f32[3,1,4,64,256]{4,3,2,0,1:T(8,128)S(1)} %bitcast.259), channel_id=1, source_target_pairs={{32,0},{64,32},{96,64},{128,96},{160,128},{192,160},{224,192},{0,2... | collective-permute-start | bytes 2359304 | tf_op jit(solution)/shard_map/ppermute | solution.py:18
  15.6 19.9 %copy-start.18 = (s32[4]{0:T(128)}, s32[4]{0:T(128)S(1)}, u32[]{:S(2)}) copy-start(s32[4]{0:T(128)S(1)} %get-tuple-element.70) | copy-start | bytes 52
  18.8 230.9 %all-reduce.5.cloned.1.call-start = ((), (), s32[]{:S(2)}) async-start(), calls=%async_computation.3 | async-start | bytes 3145728 | tf_op jit(solution)/shard_map/psum | solution.py:91
  19.2 28.2 %copy-start.19 = (pred[4]{0:T(512)(128)(4,1)}, pred[4]{0:T(512)(128)(4,1)S(1)}, u32[]{:S(2)}) copy-start(pred[4]{0:T(512)(128)(4,1)S(1)} %compare_and_fusion.2) | copy-start | bytes 16
  19.3 29.6 %copy-start.20 = (pred[4]{0:T(512)(128)(4,1)}, pred[4]{0:T(512)(128)(4,1)S(1)}, u32[]{:S(2)}) copy-start(pred[4]{0:T(512)(128)(4,1)S(1)} %compare_and_fusion.4) | copy-start | bytes 16
  19.3 30.9 %copy-start.21 = (pred[4]{0:T(512)(128)(4,1)}, pred[4]{0:T(512)(128)(4,1)S(1)}, u32[]{:S(2)}) copy-start(pred[4]{0:T(512)(128)(4,1)S(1)} %compare_and_fusion.5) | copy-start | bytes 16
  19.3 31.1 %copy-start.22 = (pred[4]{0:T(512)(128)(4,1)}, pred[4]{0:T(512)(128)(4,1)S(1)}, u32[]{:S(2)}) copy-start(pred[4]{0:T(512)(128)(4,1)S(1)} %compare_and_fusion.6) | copy-start | bytes 16
  19.4 31.2 %copy-start.23 = (pred[4]{0:T(512)(128)(4,1)}, pred[4]{0:T(512)(128)(4,1)S(1)}, u32[]{:S(2)}) copy-start(pred[4]{0:T(512)(128)(4,1)S(1)} %compare_and_fusion.7) | copy-start | bytes 16
  19.4 31.4 %copy-start.24 = (pred[4]{0:T(512)(128)(4,1)}, pred[4]{0:T(512)(128)(4,1)S(1)}, u32[]{:S(2)}) copy-start(pred[4]{0:T(512)(128)(4,1)S(1)} %compare_and_fusion.8) | copy-start | bytes 16
  19.7 31.8 %copy-start.25 = (pred[4]{0:T(512)(128)(4,1)}, pred[4]{0:T(512)(128)(4,1)S(1)}, u32[]{:S(2)}) copy-start(pred[4]{0:T(512)(128)(4,1)S(1)} %compare_and_fusion.9) | copy-start | bytes 16
  19.8 32.1 %copy-start.26 = (pred[4]{0:T(512)(128)(4,1)}, pred[4]{0:T(512)(128)(4,1)S(1)}, u32[]{:S(2)}) copy-start(pred[4]{0:T(512)(128)(4,1)S(1)} %compare_and_fusion.3) | copy-start | bytes 16
  19.8 32.3 %copy-start.27 = (f32[4]{0:T(128)}, f32[4]{0:T(128)S(1)}, u32[]{:S(2)}) copy-start(f32[4]{0:T(128)S(1)} %broadcast_subtract_fusion) | copy-start | bytes 52
  32.7 0.9 copy-start.16
  47.5 2.8 copy-start.5
  47.5 3.0 copy-start.6
  48.9 1.7 copy-start.8
  50.3 1.2 copy-start.10
  50.4 1.2 copy-start.12
  50.6 1.4 copy-start.13
  52.1 1.6 copy-start.2
  55.3 3.9 %copy-start.33 = (s32[64]{0:T(128)S(1)}, s32[64]{0:T(128)}, u32[]{:S(2)}) copy-start(s32[64]{0:T(128)} %param.13) | copy-start | bytes 772
  55.4 5.0 %copy-start.32 = (s32[4]{0:T(128)S(1)}, s32[4]{0:T(128)}, u32[]{:S(2)}) copy-start(s32[4]{0:T(128)} %param.14) | copy-start | bytes 52
  59.3 0.5 copy-start.31
  112.2 142.2 %copy-start.3 = (f32[4,3,64,256]{3,2,1,0:T(8,128)S(1)}, f32[4,3,64,256]{3,2,1,0:T(8,128)}, u32[]{:S(2)}) copy-start(f32[4,3,64,256]{3,2,1,0:T(8,128)} %gather_fusion.7) | copy-start | bytes 2359300
  112.2 142.2 %copy-start.4 = (f32[4,3,64,256]{3,2,1,0:T(8,128)S(1)}, f32[4,3,64,256]{3,2,1,0:T(8,128)}, u32[]{:S(2)}) copy-start(f32[4,3,64,256]{3,2,1,0:T(8,128)} %gather_fusion.5) | copy-start | bytes 2359300
  249.7 4.7 %copy-start.7 = (f32[4,3,64,256]{3,2,1,0:T(8,128)S(1)}, f32[4,3,64,256]{3,2,1,0:T(8,128)}, u32[]{:S(2)}) copy-start(f32[4,3,64,256]{3,2,1,0:T(8,128)} %gather_fusion.3) | copy-start | bytes 2359300
  249.7 4.7 %copy-start.9 = (f32[4,3,64,256]{3,2,1,0:T(8,128)S(1)}, f32[4,3,64,256]{3,2,1,0:T(8,128)}, u32[]{:S(2)}) copy-start(f32[4,3,64,256]{3,2,1,0:T(8,128)} %gather_fusion.2) | copy-start | bytes 2359300
  249.7 4.7 %copy-start.11 = (f32[4,3,64,256]{3,2,1,0:T(8,128)S(1)}, f32[4,3,64,256]{3,2,1,0:T(8,128)}, u32[]{:S(2)}) copy-start(f32[4,3,64,256]{3,2,1,0:T(8,128)} %gather_fusion.1) | copy-start | bytes 2359300
  249.7 4.7 %copy-start.14 = (f32[3,1,4,64,128]{4,3,2,1,0:T(8,128)S(1)}, f32[3,1,4,64,128]{4,3,2,1,0:T(8,128)}, u32[]{:S(2)}) copy-start(f32[3,1,4,64,128]{4,3,2,1,0:T(8,128)} %param.10) | copy-start | bytes 1179652
  249.7 4.7 %copy-start.15 = (f32[4,64,256]{2,1,0:T(8,128)S(1)}, f32[4,64,256]{2,1,0:T(8,128)}, u32[]{:S(2)}) copy-start(f32[4,64,256]{2,1,0:T(8,128)} %get-tuple-element.40) | copy-start | bytes 786436
  262.1 1.1 copy-start.30
  296.2 20.6 %all-to-all-start.1 = ((f32[3,1,4,64,128]{4,2,0,1,3:T(4,128)}), f32[3,1,4,64,128]{4,2,0,1,3:T(4,128)S(1)}, u32[]{:S(2)}, u32[]{:S(2)}) async-start(f32[3,1,4,64,128]{4,2,0,1,3:T(4,128)} %reshape.459), calls=%async_computation.1 | async-start | bytes 786432 | tf_op jit(solution)/shard_map/all_to_all | solution.py:113
Sparse Core Ops, SparseCore 0:
  18.9 76.5 all-reduce.2
  98.9 150.7 all-reduce.4
where the time goes:
time: 328 us; the launch traced here: 327 us
  waiting for transfers between devices  196 us (60%)
  local copies, waits for them, and re-layouts  50.8 us (15%)
  blocking collectives  27.5 us (8%)
  matrix products  17.6 us (5%)
  between operations  14.4 us (4%)
  starting transfers between devices  12.1 us (4%)
  other arithmetic  8.77 us (3%)
    psum x1, waiting for transfers between devices, local(): summed = lax.psum(stress, ('kx', 'real'))  134 us
    psum x1, waiting for transfers between devices, local(): low_fields = lax.psum(own_low, 'kx')  35.1 us
    all_to_all x1, blocking collectives, local(): lax.all_to_all(flat_out, ('kx', 'ht'), split_axis=3, concat_axis=3, tiled...  27.5 us
    all_to_all x1, waiting for transfers between devices, local(): lax.all_to_all(applied, ('kx', 'ht'), split_axis=3, concat_axis=3, tiled=...  14.2 us
    ppermute x1, waiting for transfers between devices, extended_2(): lax.ppermute(lax.slice_in_dim(block, block.shape[dim] - width, None, axis...  12.9 us
    gather x8, local copies, waits for them, and re-layouts, local(): partner = jnp.take(extended, local_partner[:, member], axis=2)  12 us
    unnamed x84, local copies, waits for them, and re-layouts  11.8 us
    slice x1, local copies, waits for them, and re-layouts, local(): low_one = low_fields[:, :, member:member + 1]  7.67 us
  transfers between devices with their start and end apart: 5, of which 4 were waited for; matrix products, arithmetic and copies ran while one was open for 15% of the time, Pallas kernels for 0%

commit v1 on v0

--- a/solution.py
+++ b/solution.py
@@ -88,7 +88,7 @@
         stresses.append(jnp.sum(weighted, axis=(1, 2)))
     stress = jnp.stack(stresses, axis=1)
     nonlinear = jnp.dot(high_low, backward, precision=highest)
-    summed = lax.psum(stress, ("kx", "real"))
+    summed = lax.psum(lax.psum(stress, axis_name="real"), "kx")
     low_forcing = jnp.dot(summed / realizations, backward, precision=highest)
     forcing = nonlinear * high_mask[None, None, :, None, None]
     forcing = (

time: 328 us -> 300 us (0.915)
  waiting for transfers between devices: 196 us -> 177 us
  other arithmetic: 8.77 us -> 20.8 us
  local copies, waits for them, and re-layouts: 50.8 us -> 40.8 us
  matrix products: 17.6 us -> 11.3 us
  blocking collectives: 27.5 us -> 23.4 us
    psum x1, waiting for transfers between devices: 134 us -> 53.4 us  [local(): summed = lax.psum(lax.psum(stress, axis_name='real'), 'kx')]
    psum x1, waiting for transfers between devices: 35.1 us -> 93.7 us  [local(): low_fields = lax.psum(own_low, 'kx')]
    unnamed x84 -> x78, local copies, waits for them, and re-layouts: 11.8 us -> 1.48 us
    select_n x16, other arithmetic: 3.58 us -> 9.24 us  [local(): partner = jnp.take(extended, local_partner[:, member], axis=2)]
    mul x1 -> x8, other arithmetic: 1.39 us -> 5.86 us  [local(): high_low = high_low + low_one * partner[1:2] + partner * low_one[1:2]]
    all_to_all x1, blocking collectives: 27.5 us -> 23.4 us  [local(): lax.all_to_all(flat_out, ('kx', 'ht'), split_axis=3, concat_axis=3, tiled...]
    dot_general x1, matrix products: 5.87 us -> 2.44 us  [local(): nonlinear = jnp.dot(high_low, backward, precision=highest)]
  transfers between devices with their start and end apart: 5 -> 5, of which waited for: 4 -> 4; matrix products, arithmetic and copies ran while one was open for 15% -> 2% of each run, Pallas kernels for 0% -> 0%
where the time goes in v1:
time: 300 us; the launch traced here: 299 us
  waiting for transfers between devices  177 us (59%)
  local copies, waits for them, and re-layouts  40.8 us (14%)
  blocking collectives  23.4 us (8%)
  other arithmetic  20.8 us (7%)
  between operations  14.4 us (5%)
  starting transfers between devices  12.2 us (4%)
  matrix products  11.3 us (4%)
    psum x1, waiting for transfers between devices, local(): low_fields = lax.psum(own_low, 'kx')  93.7 us
    psum x1, waiting for transfers between devices, local(): summed = lax.psum(lax.psum(stress, axis_name='real'), 'kx')  53.4 us
    all_to_all x1, blocking collectives, local(): lax.all_to_all(flat_out, ('kx', 'ht'), split_axis=3, concat_axis=3, tiled...  23.4 us
    ppermute x1, waiting for transfers between devices, extended_2(): lax.ppermute(lax.slice_in_dim(block, block.shape[dim] - width, None, axis...  14.9 us
    all_to_all x1, waiting for transfers between devices, local(): lax.all_to_all(applied, ('kx', 'ht'), split_axis=3, concat_axis=3, tiled=...  14.3 us
    gather x8, local copies, waits for them, and re-layouts, local(): partner = jnp.take(extended, local_partner[:, member], axis=2)  12 us
    select_n x16, other arithmetic, local(): partner = jnp.take(extended, local_partner[:, member], axis=2)  9.24 us
    slice x1, local copies, waits for them, and re-layouts, local(): low_one = low_fields[:, :, member:member + 1]  7.66 us
  transfers between devices with their start and end apart: 5, of which 4 were waited for; matrix products, arithmetic and copies ran while one was open for 2% of the time, Pallas kernels for 0%

profile of v1, /device:TPU:1, one launch (start us, length us, event | category | flops | bytes accessed | tf_op | source)
XLA Modules:
  0.0 299.5 jit_solution(11660636074015779274)
XLA Ops:
  6.6 2.4 fusion.12
  9.0 2.5 collective-permute-start
  11.5 4.0 %collective-permute-start.1 = (f32[3,1,4,64,256]{4,3,2,0,1:T(8,128)S(1)}, f32[3,1,4,64,256]{4,3,2,0,1:T(8,128)}, u32[]{:S(2)}, u32[]{:S(2)}) collective-permute-start(f32[3,1,4,64,256]{4,3,2,0,1:T(8,128)S(1)} %bitcast.259), channel_id=1, source_target_pairs={{32,0},{64,32},{96,64},{128,96},{160,128},{192,160},{224,192},{0,2... | collective-permute-start | bytes 2359304 | tf_op jit(solution)/shard_map/ppermute | solution.py:18
  16.9 0.8 fusion.38
  17.8 14.9 %collective-permute-done = f32[3,1,4,64,256]{4,3,2,0,1:T(8,128)S(1)} collective-permute-done((f32[3,1,4,64,256]{4,3,2,0,1:T(8,128)S(1)}, f32[3,1,4,64,256]{4,3,2,0,1:T(8,128)S(1)}, u32[]{:S(2)}, u32[]{:S(2)}) %collective-permute-start) | collective-permute-done | bytes 786464 | tf_op jit(solution)/shard_map/ppermute | solution.py:15
  32.7 0.9 copy-done.27
  33.6 1.8 maximum_bitcast_fusion
  35.4 1.5 gather_fusion
  36.9 1.5 gather_fusion.1
  38.3 1.3 bitcast_select_fusion.9
  39.7 0.8 slice_bitcast_fusion.7
  40.7 0.8 slice_bitcast_fusion.6
  41.5 1.5 gather_fusion.2
  43.0 1.3 bitcast_select_fusion.7
  44.3 0.8 slice_bitcast_fusion.5
  45.1 1.6 gather_fusion.3
  46.7 1.3 bitcast_select_fusion.6
  48.0 0.8 slice_bitcast_fusion.4
  48.8 1.5 gather_fusion.4
  50.3 1.3 bitcast_select_fusion.5
  51.5 0.8 slice_bitcast_fusion.3
  52.4 1.5 gather_fusion.5
  53.9 1.3 bitcast_select_fusion.4
  55.1 0.8 slice_bitcast_fusion.2
  56.0 1.5 gather_fusion.6
  57.5 1.3 bitcast_select_fusion.3
  58.7 0.8 slice_bitcast_fusion.1
  59.6 1.5 gather_fusion.7
  61.1 1.4 bitcast_select_fusion.2
  62.9 1.6 multiply_reduce_fusion
  65.5 0.8 stack.34
  66.3 4.8 %stack.35 = f32[3,8,64,256]{3,1,2,0:T(8,128)} concatenate(f32[3,1,64,256]{3,1,2,0:T(1,128)S(1)} %stack.27, f32[3,1,64,256]{3,1,2,0:T(1,128)S(1)} %stack.28, f32[3,1,64,256]{3,1,2,0:T(1,128)S(1)} %stack.29, f32[3,1,64,256]{3,1,2,0:T(1,128)S(1)} %stack.30, f32[3,1,64,256]{3,1,2,0:T(1,128)S(1)} %stack.31, f32[3,1,64,256]{3,1,2,0:T(1,128)S(1)} %stack.32, ...), dimensions={1} | concatenate | bytes 3145728 | tf_op jit(solution)/shard_map/stack | solution.py:89
  71.5 2.5 convolution_bitcast_fusion
  73.9 53.4 %all-reduce.4.cloned.1.call-done = f32[3,8,64,256]{3,1,2,0:T(8,128)} async-done(((f32[3,8,64,256]{3,1,2,0:T(8,128)}), f32[3,8,64,256]{3,1,2,0:T(8,128)}) %all-reduce.4.cloned.1.call-update) | async-done | bytes 1572880 | tf_op jit(solution)/shard_map/psum | solution.py:91
  127.6 93.7 %all-reduce.6.cloned.1.call-done = (f32[3,1,8,64,256]{4,2,3,0,1:T(8,128)}, f32[3,8,64,256]{3,1,2,0:T(8,128)}) async-done(((f32[3,1,8,64,256]{4,2,3,0,1:T(8,128)}, f32[3,8,64,256]{3,1,2,0:T(8,128)}), (f32[3,1,8,64,256]{4,2,3,0,1:T(8,128)}, f32[3,8,64,256]{3,1,2,0:T(8,128)})) %all-reduce.6.cloned.1.call-update) | async-done | bytes 3145744 | tf_op jit(solution)/shard_map/psum | solution.py:80
  221.3 7.7 %fusion.51 = (f32[3,1,1,64,256]{4,2,3,0,1:T(1,128)S(1)}, f32[3,1,1,64,256]{4,2,3,0,1:T(1,128)S(1)}, f32[3,1,1,64,256]{4,2,3,0,1:T(1,128)S(1)}, f32[3,1,1,64,256]...) fusion(f32[3,1,8,64,256]{4,2,3,0,1:T(8,128)} %get-tuple-element.23), kind=kLoop, calls=%fused_computation.172 | loop fusion | bytes 3145728 | tf_op jit(solution)/shard_map/slice | solution.py:85
  229.0 3.3 %fusion.52 = (f32[1,1,1,64,256]{4,2,3,0,1:T(1,128)S(1)}, f32[1,1,1,64,256]{4,2,3,0,1:T(1,128)S(1)}, f32[1,1,1,64,256]{4,2,3,0,1:T(1,128)S(1)}, f32[1,1,1,64,256]...) fusion(f32[3,1,8,64,256]{4,2,3,0,1:T(8,128)} %get-tuple-element.23), kind=kLoop, calls=%fused_computation.173 | loop fusion | bytes 1048576 | tf_op jit(solution)/shard_map/slice | solution.py:86
  232.6 1.9 fusion
  235.4 2.4 fusion.6
  238.6 1.0 gather_fusion.8
  240.9 23.4 %all_to_all.10 = f32[3,1,4,64,128]{4,2,0,1,3:T(4,128)S(1)} all-to-all(f32[3,1,4,64,128]{4,2,0,1,3:T(4,128)S(1)} %reshape.457), channel_id=1, replica_groups=mesh['kx'=8,'ht'=8,'real'=4] {'kx','ht'}, dimensions={3} | all-to-all | bytes 786432 | tf_op jit(solution)/shard_map/all_to_all | solution.py:106
  265.2 1.5 convolution_bitcast_fusion.1
  267.3 1.3 reshape.459
  268.6 5.5 %all-to-all-start.1 = ((f32[3,1,4,64,128]{4,2,0,1,3:T(4,128)}), f32[3,1,4,64,128]{4,2,0,1,3:T(4,128)S(1)}, u32[]{:S(2)}, u32[]{:S(2)}) async-start(f32[3,1,4,64,128]{4,2,0,1,3:T(4,128)} %reshape.459), calls=%async_computation.1 | async-start | bytes 786432 | tf_op jit(solution)/shard_map/all_to_all | solution.py:113
  274.0 0.8 scatter_custom_fusion
  274.9 14.3 %all-to-all-done.1 = f32[3,1,4,64,128]{4,2,0,1,3:T(4,128)S(1)} async-done(((f32[3,1,4,64,128]{4,2,0,1,3:T(4,128)}), f32[3,1,4,64,128]{4,2,0,1,3:T(4,128)S(1)}, u32[]{:S(2)}, u32[]{:S(2)}) %all-to-all-start.1) | async-done | bytes 393248 | tf_op jit(solution)/shard_map/all_to_all | solution.py:113
  289.9 1.1 gather_fusion.9
  291.6 1.0 copy.49
  (146 shorter events, 8.6 us)
Async XLA Ops:
  6.5 258.6 %copy-start = (f32[1,512,512]{2,1,0:T(8,128)S(1)}, f32[1,512,512]{2,1,0:T(8,128)}, u32[]{:S(2)}) copy-start(f32[1,512,512]{2,1,0:T(8,128)} %param.15) | copy-start | bytes 3145732
  6.5 120.9 %all-reduce.4.cloned.1.call-start = ((), (), s32[]{:S(2)}) async-start(), calls=%async_computation.2 | async-start | bytes 3145728 | tf_op jit(solution)/shard_map/psum | solution.py:91
  9.0 23.7 %copy-start.1 = (f32[256,3,4,64]{0,3,2,1:T(8,128)}, f32[256,3,4,64]{0,3,2,1:T(8,128)S(1)}, u32[]{:S(2)}) copy-start(f32[256,3,4,64]{0,3,2,1:T(8,128)S(1)} %fusion.12) | copy-start | bytes 2359300
  9.0 23.7 %collective-permute-start = (f32[3,1,4,64,256]{4,3,2,0,1:T(8,128)S(1)}, f32[3,1,4,64,256]{4,3,2,0,1:T(8,128)S(1)}, u32[]{:S(2)}, u32[]{:S(2)}) collective-permute-start(f32[3,1,4,64,256]{4,3,2,0,1:T(8,128)S(1)} %bitcast.258), channel_id=1, source_target_pairs={{0,32},{32,64},{64,96},{96,128},{128,160},{160,192},{192,224},{224... | collective-permute-start | bytes 2359304 | tf_op jit(solution)/shard_map/ppermute | solution.py:15
  11.5 22.1 %collective-permute-start.1 = (f32[3,1,4,64,256]{4,3,2,0,1:T(8,128)S(1)}, f32[3,1,4,64,256]{4,3,2,0,1:T(8,128)}, u32[]{:S(2)}, u32[]{:S(2)}) collective-permute-start(f32[3,1,4,64,256]{4,3,2,0,1:T(8,128)S(1)} %bitcast.259), channel_id=1, source_target_pairs={{32,0},{64,32},{96,64},{128,96},{160,128},{192,160},{224,192},{0,2... | collective-permute-start | bytes 2359304 | tf_op jit(solution)/shard_map/ppermute | solution.py:18
  32.7 0.9 copy-start.27
  38.3 2.2 copy-start.4
  61.0 1.6 copy-start.2
  61.0 1.6 copy-start.21
  61.0 1.6 copy-start.22
  61.0 1.6 copy-start.23
  61.1 1.6 copy-start.24
  61.1 1.7 copy-start.25
  61.1 1.8 copy-start.26
  66.3 5.1 %copy-start.28 = (s32[8]{0:T(128)S(1)}, s32[8]{0:T(128)}, u32[]{:S(2)}) copy-start(s32[8]{0:T(128)} %param.11) | copy-start | bytes 100
  71.2 150.1 %all-reduce.6.cloned.1.call-start = ((), (), s32[]{:S(2)}) async-start(), calls=%async_computation.3 | async-start | bytes 6291456 | tf_op jit(solution)/shard_map/psum | solution.py:80
  71.4 56.0 %copy-start.30 = (s32[64]{0:T(128)S(1)}, s32[64]{0:T(128)}, u32[]{:S(2)}) copy-start(s32[64]{0:T(128)} %param.13) | copy-start | bytes 772
  71.4 56.0 %copy-start.29 = (s32[4]{0:T(128)S(1)}, s32[4]{0:T(128)}, u32[]{:S(2)}) copy-start(s32[4]{0:T(128)} %param.14) | copy-start | bytes 52
  221.3 13.8 %copy-start.16 = (f32[4,64,256]{2,1,0:T(8,128)S(1)}, f32[4,64,256]{2,1,0:T(8,128)}, u32[]{:S(2)}) copy-start(f32[4,64,256]{2,1,0:T(8,128)} %get-tuple-element.45) | copy-start | bytes 786436
  221.3 13.9 %copy-start.17 = (f32[4,64,256]{2,1,0:T(8,128)S(1)}, f32[4,64,256]{2,1,0:T(8,128)}, u32[]{:S(2)}) copy-start(f32[4,64,256]{2,1,0:T(8,128)} %get-tuple-element.47) | copy-start | bytes 786436
  221.3 13.9 %copy-start.18 = (f32[4,64,256]{2,1,0:T(8,128)S(1)}, f32[4,64,256]{2,1,0:T(8,128)}, u32[]{:S(2)}) copy-start(f32[4,64,256]{2,1,0:T(8,128)} %get-tuple-element.49) | copy-start | bytes 786436
  221.3 13.9 %copy-start.19 = (f32[4,64,256]{2,1,0:T(8,128)S(1)}, f32[4,64,256]{2,1,0:T(8,128)}, u32[]{:S(2)}) copy-start(f32[4,64,256]{2,1,0:T(8,128)} %get-tuple-element.51) | copy-start | bytes 786436
  221.3 13.9 %copy-start.20 = (f32[4,64,256]{2,1,0:T(8,128)S(1)}, f32[4,64,256]{2,1,0:T(8,128)}, u32[]{:S(2)}) copy-start(f32[4,64,256]{2,1,0:T(8,128)} %get-tuple-element.53) | copy-start | bytes 786436
  229.0 3.6 %copy-start.13 = (f32[3,8,64,256]{3,1,2,0:T(8,128)S(1)}, f32[3,8,64,256]{3,1,2,0:T(8,128)}, u32[]{:S(2)}) copy-start(f32[3,8,64,256]{3,1,2,0:T(8,128)} %get-tuple-element.24) | copy-start | bytes 4718596
  232.3 2.9 copy-start.15
  232.3 2.9 copy-start.12
  232.4 2.8 copy-start.11
  232.4 2.8 copy-start.10
  232.5 2.8 copy-start.9
  232.5 2.7 copy-start.3
  232.5 2.7 copy-start.5
  232.5 2.7 copy-start.6
  232.5 2.7 copy-start.7
  232.6 2.8 copy-start.8
  232.6 2.8 copy-start.14
  268.6 20.6 %all-to-all-start.1 = ((f32[3,1,4,64,128]{4,2,0,1,3:T(4,128)}), f32[3,1,4,64,128]{4,2,0,1,3:T(4,128)S(1)}, u32[]{:S(2)}, u32[]{:S(2)}) async-start(f32[3,1,4,64,128]{4,2,0,1,3:T(4,128)} %reshape.459), calls=%async_computation.1 | async-start | bytes 786432 | tf_op jit(solution)/shard_map/all_to_all | solution.py:113
Sparse Core Ops, SparseCore 0:
  71.3 56.0 all-reduce.3
  129.8 91.4 all-reduce.5
